TPU v7x, 128 devices: a whole 4x4x4 slice. The times are simulated.
128 devices in a mesh: member: 2 (over y_hi), gridy: 8 (over x, core), gridx: 8 (over z, y_lo).
Axes of the slice: x: 4, y: 4 (y_hi: 2, y_lo: 2; y = y_hi * 2 + y_lo), z: 4, core: 2. Of those that a mesh axis runs over, the one named last changes fastest.
Arguments:
- temp: float32 [4, 4, 512, 2048], P('member', None, 'gridy', 'gridx'), may hold values from -6 to 6
- salt: float32 [4, 4, 512, 2048], P('member', None, 'gridy', 'gridx'), may hold values from -6 to 6
- uvel: float32 [4, 4, 512, 2048], P('member', None, 'gridy', 'gridx'), may hold values from -3 to 3
- vvel: float32 [4, 4, 512, 2048], P('member', None, 'gridy', 'gridx'), may hold values from -3 to 3
- eta: float32 [4, 512, 2048], P('member', 'gridy', 'gridx'), may hold values from -6 to 6
- land_mask: int32 [512, 2048], P('gridy', 'gridx'), may hold values 0 or 1
- clone_source: int32 [4], P('member'), may hold values from 0 to 3
Outputs:
- new_temp: float32 [4, 4, 512, 2048], P('member', None, 'gridy', 'gridx')
- new_salt: float32 [4, 4, 512, 2048], P('member', None, 'gridy', 'gridx')
- new_uvel: float32 [4, 4, 512, 2048], P('member', None, 'gridy', 'gridx')
- new_vvel: float32 [4, 4, 512, 2048], P('member', None, 'gridy', 'gridx')
- new_eta: float32 [4, 512, 2048], P('member', 'gridy', 'gridx')
- overturning: float32 [4, 4, 512], P('member', None, 'gridy')
- clone_weight: float32 [4], P('member')
All inputs are finite; a program needn't handle non-finite values. No bound on the sum of `land_mask` on one device may be relied on, other than what follows from the above.
Results may differ from a plain program's by a relative error of at most 0.0001.
Values sent between devices are 32-bit elements; how exact they have to be, the bound alone decides.
A program may use at most 128 MiB of HBM per device.

v0:
```python
import jax
import jax.numpy as jnp
from jax import lax
from jax.sharding import PartitionSpec as P

STEPS = 2
ITERS = 3
ALPHA_T = 0.8
BETA_S = 0.6
PRESS_K = 0.25
STEP_DT = 0.1
KAPPA = 0.1
VISCOSITY = 0.1
DRAG_K = 0.05
CORI_K = 1.0
SURF_C = 4.0
DIV_K = 0.5
GRAV_K = 0.5


def padded_2(block, sides, width):
    for axis, dim in sides:
        count = lax.axis_size(axis)
        forward = [(i, i + 1) for i in range(count - 1)]
        forward.append((count - 1, 0))
        backward = [(target, source) for source, target in forward]
        low = lax.ppermute(
            lax.slice_in_dim(block, block.shape[dim] - width, None, axis=dim), axis, forward
        )
        high = lax.ppermute(lax.slice_in_dim(block, 0, width, axis=dim), axis, backward)
        block = jnp.concatenate([low, block, high], axis=dim)
    return block


def pressure(temp, salt):
    return PRESS_K * jnp.cumsum(BETA_S * salt - ALPHA_T * temp, axis=-3)


def split_rims(padded, south_keep, north_keep):
    east_side = padded[..., 1:-1, 2:]
    west_side = padded[..., 1:-1, :-2]
    north_side = padded[..., 2:, 1:-1]
    south_side = padded[..., :-2, 1:-1]
    north_side = north_side.at[..., -1, :].multiply(north_keep)
    south_side = south_side.at[..., 0, :].multiply(south_keep)
    return (east_side, west_side, north_side, south_side)


def volume_sides(fields, south_keep, north_keep):
    padded = padded_2(jnp.stack(fields), (("gridy", 3), ("gridx", 4)), 1)
    return split_rims(padded, south_keep, north_keep)


def surface_sides(fields, south_keep, north_keep):
    padded = padded_2(jnp.stack(fields), (("gridy", 2), ("gridx", 3)), 1)
    return split_rims(padded, south_keep, north_keep)


def surface_apply(field, south_keep, north_keep):
    east_side, west_side, north_side, south_side = surface_sides((field,), south_keep, north_keep)
    return (1.0 + 4.0 * SURF_C) * field - SURF_C * (
        east_side[0] + west_side[0] + north_side[0] + south_side[0]
    )


def member_total(values):
    return jnp.sum(values, axis=(1, 2))


def squared_norm(residual):
    return lax.psum(member_total(residual * residual), ("gridy", "gridx"))


def widen(values):
    return values[:, None, None]


def surface_solve(rhs, south_keep, north_keep):
    solution = jnp.zeros_like(rhs)
    residual = rhs
    direction = rhs
    norm_now = squared_norm(residual)
    for count in range(ITERS):
        image = surface_apply(direction, south_keep, north_keep)
        alpha = norm_now / lax.psum(member_total(direction * image), ("gridy", "gridx"))
        solution = solution + widen(alpha) * direction
        residual = residual - widen(alpha) * image
        norm_next = squared_norm(residual)
        direction = residual + widen(norm_next / norm_now) * direction
        norm_now = norm_next
    return solution


def shards(temp, salt, uvel, vvel, eta, land_mask, clone_source):
    levels = temp.shape[1]
    rows = temp.shape[2]
    cols = temp.shape[3]
    ocean = land_mask.astype(jnp.float32)
    tile_row = lax.axis_index("gridy")
    tile_count = lax.axis_size("gridy")
    total_rows = rows * tile_count
    total_cols = cols * lax.axis_size("gridx")
    south_keep = (tile_row > 0).astype(jnp.float32)
    north_keep = (tile_row < tile_count - 1).astype(jnp.float32)
    latitude = (tile_row * rows + jnp.arange(rows, dtype=jnp.int32)).astype(jnp.float32) + 0.5
    coriolis = (CORI_K * (2.0 * latitude / total_rows - 1.0))[:, None]
    for count in range(STEPS):
        press = pressure(temp, salt)
        east_side, west_side, north_side, south_side = volume_sides(
            (temp, salt, uvel, vvel, press), south_keep, north_keep
        )
        lap_temp = east_side[0] + west_side[0] + north_side[0] + south_side[0] - 4.0 * temp
        lap_salt = east_side[1] + west_side[1] + north_side[1] + south_side[1] - 4.0 * salt
        lap_uvel = east_side[2] + west_side[2] + north_side[2] + south_side[2] - 4.0 * uvel
        lap_vvel = east_side[3] + west_side[3] + north_side[3] + south_side[3] - 4.0 * vvel
        temp_next = ocean * (
            temp
            - STEP_DT
            * 0.5
            * (uvel * (east_side[0] - west_side[0]) + vvel * (north_side[0] - south_side[0]))
            + KAPPA * lap_temp
        )
        salt_next = ocean * (
            salt
            - STEP_DT
            * 0.5
            * (uvel * (east_side[1] - west_side[1]) + vvel * (north_side[1] - south_side[1]))
            + KAPPA * lap_salt
        )
        ustar = ocean * (
            uvel
            + STEP_DT * (coriolis * vvel - 0.5 * (east_side[4] - west_side[4]) - DRAG_K * uvel)
            + VISCOSITY * lap_uvel
        )
        vstar = ocean * (
            vvel
            + STEP_DT * (-coriolis * uvel - 0.5 * (north_side[4] - south_side[4]) - DRAG_K * vvel)
            + VISCOSITY * lap_vvel
        )
        trans_u = jnp.sum(ustar, axis=1)
        trans_v = jnp.sum(vstar, axis=1)
        east_t, west_t, north_t, south_t = surface_sides((trans_u, trans_v), south_keep, north_keep)
        rhs = eta - DIV_K * 0.5 * (east_t[0] - west_t[0] + (north_t[1] - south_t[1]))
        eta = surface_solve(rhs, south_keep, north_keep)
        east_e, west_e, north_e, south_e = surface_sides((eta,), south_keep, north_keep)
        uvel = ocean * (ustar - GRAV_K * 0.5 * (east_e[0] - west_e[0])[:, None])
        vvel = ocean * (vstar - GRAV_K * 0.5 * (north_e[0] - south_e[0])[:, None])
        temp = temp_next
        salt = salt_next
    zonal_scale = 1.0 / jnp.sqrt(jnp.float32(total_cols))
    score_scale = 1.0 / jnp.sqrt(jnp.float32(levels * total_rows))
    lat_weight = latitude / total_rows
    zonal_local = jnp.sum(vvel, axis=3)
    zonal_whole = lax.psum(zonal_local, "gridx")
    overturn = jnp.cumsum(zonal_whole, axis=1) * zonal_scale
    score = lax.psum(jnp.sum(overturn * lat_weight, axis=(1, 2)) * score_scale, "gridy")
    state_stack = jnp.stack((temp, salt, uvel, vvel))
    every_state, every_eta, every_score = (
        lax.all_gather(state_stack, "member", axis=1, tiled=True),
        lax.all_gather(eta, "member", axis=0, tiled=True),
        lax.all_gather(score, "member", axis=0, tiled=True),
    )
    picked = jnp.take(every_state, clone_source, axis=1)
    new_eta = jnp.take(every_eta, clone_source, axis=0)
    clone_weight = jnp.take(every_score, clone_source, axis=0) - jnp.mean(every_score)
    return (picked[0], picked[1], picked[2], picked[3], new_eta, overturn, clone_weight)


def solution(mesh):
    in_specs = (
        P("member", None, "gridy", "gridx"),
        P("member", None, "gridy", "gridx"),
        P("member", None, "gridy", "gridx"),
        P("member", None, "gridy", "gridx"),
        P("member", "gridy", "gridx"),
        P("gridy", "gridx"),
        P("member"),
    )
    out_specs = (
        P("member", None, "gridy", "gridx"),
        P("member", None, "gridy", "gridx"),
        P("member", None, "gridy", "gridx"),
        P("member", None, "gridy", "gridx"),
        P("member", "gridy", "gridx"),
        P("member", None, "gridy"),
        P("member"),
    )
    return jax.shard_map(shards, mesh=mesh, in_specs=in_specs, out_specs=out_specs, check_vma=False)
```

profile of v0, /device:TPU:1, one launch (start us, length us, event | category | flops | bytes accessed | tf_op | source)
XLA Modules:
  0.0 1724.0 jit_solution(7264022242541431259)
XLA Ops:
  43.6 4.2 collective-permute-start.5
  62.0 3.9 collective-permute-start.10
  68.0 133.2 %all-reduce.2 = (f32[2]{0:T(128)S(1)}, f32[2]{0:T(128)S(1)}) all-reduce(f32[2]{0:T(128)S(1)} %get-tuple-element.298, f32[2]{0:T(128)S(1)} %get-tuple-element.297), channel_id=1, replica_groups=mesh['member'=2,'gridy'=8,'gridx'=8] {'gridy','gridx'}, use_global_device_ids=true, to_apply=%region_4.5 | all-reduce | flops 4 | bytes 32 | tf_op jit(solution)/shard_map/psum | solution.py:71
  201.4 139.0 %psum.100 = f32[2]{0:T(128)S(1)} all-reduce(f32[2]{0:T(128)S(1)} %get-tuple-element.316), channel_id=1, replica_groups=mesh['member'=2,'gridy'=8,'gridx'=8] {'gridy','gridx'}, use_global_device_ids=true, to_apply=%region_8.9 | all-reduce | flops 2 | bytes 16 | tf_op jit(solution)/shard_map/psum | solution.py:71
  340.5 11.4 collective-permute-start.13
  358.8 133.5 %psum.101 = f32[2]{0:T(128)S(1)} all-reduce(f32[2]{0:T(128)S(1)} %get-tuple-element.314), channel_id=1, replica_groups=mesh['member'=2,'gridy'=8,'gridx'=8] {'gridy','gridx'}, use_global_device_ids=true, to_apply=%region_10.11 | all-reduce | flops 2 | bytes 16 | tf_op jit(solution)/shard_map/psum | solution.py:85
  492.5 139.0 %psum.102 = f32[2]{0:T(128)S(1)} all-reduce(f32[2]{0:T(128)S(1)} %multiply_reduce_fusion.5), channel_id=1, replica_groups=mesh['member'=2,'gridy'=8,'gridx'=8] {'gridy','gridx'}, use_global_device_ids=true, to_apply=%region_12.13 | all-reduce | flops 2 | bytes 16 | tf_op jit(solution)/shard_map/psum | solution.py:71
  632.1 11.4 collective-permute-start.17
  654.5 134.3 %psum.103 = f32[2]{0:T(128)} all-reduce(f32[2]{0:T(128)} %fusion.143), channel_id=1, replica_groups=mesh['member'=2,'gridy'=8,'gridx'=8] {'gridy','gridx'}, use_global_device_ids=true, to_apply=%region_14.15 | all-reduce | flops 2 | bytes 16 | tf_op jit(solution)/shard_map/psum | solution.py:85
  790.5 11.7 collective-permute-start.21
  816.5 4.1 collective-permute-start.25
  883.2 131.9 %all-reduce.1 = (f32[2]{0:T(128)}, f32[2]{0:T(128)}) all-reduce(f32[2]{0:T(128)} %get-tuple-element.296, f32[2]{0:T(128)} %get-tuple-element.295), channel_id=1, replica_groups=mesh['member'=2,'gridy'=8,'gridx'=8] {'gridy','gridx'}, use_global_device_ids=true, to_apply=%region_19.20 | all-reduce | flops 4 | bytes 32 | tf_op jit(solution)/shard_map/psum | solution.py:71
  1017.1 140.1 %psum.106 = f32[2]{0:T(128)S(1)} all-reduce(f32[2]{0:T(128)} %get-tuple-element.307), channel_id=1, replica_groups=mesh['member'=2,'gridy'=8,'gridx'=8] {'gridy','gridx'}, use_global_device_ids=true, to_apply=%region_23.24 | all-reduce | flops 2 | bytes 16 | tf_op jit(solution)/shard_map/psum | solution.py:71
  1158.9 11.7 collective-permute-start.37
  1183.0 131.7 %psum.107 = f32[2]{0:T(128)} all-reduce(f32[2]{0:T(128)} %get-tuple-element.305), channel_id=1, replica_groups=mesh['member'=2,'gridy'=8,'gridx'=8] {'gridy','gridx'}, use_global_device_ids=true, to_apply=%region_25.26 | all-reduce | flops 2 | bytes 16 | tf_op jit(solution)/shard_map/psum | solution.py:85
  1317.6 141.2 %psum.108 = f32[2]{0:T(128)} all-reduce(f32[2]{0:T(128)} %multiply_reduce_fusion), channel_id=1, replica_groups=mesh['member'=2,'gridy'=8,'gridx'=8] {'gridy','gridx'}, use_global_device_ids=true, to_apply=%region_27.28 | all-reduce | flops 2 | bytes 16 | tf_op jit(solution)/shard_map/psum | solution.py:71
  1460.6 11.8 collective-permute-start.41
  1484.5 131.7 %psum.109 = f32[2]{0:T(128)} all-reduce(f32[2]{0:T(128)} %fusion.107), channel_id=1, replica_groups=mesh['member'=2,'gridy'=8,'gridx'=8] {'gridy','gridx'}, use_global_device_ids=true, to_apply=%region_29.30 | all-reduce | flops 2 | bytes 16 | tf_op jit(solution)/shard_map/psum | solution.py:85
  1617.8 11.5 collective-permute-start.45
  1648.0 16.1 psum.110
  1664.8 9.2 all_gather.10
  1674.0 21.4 %psum.111 = f32[2]{0:T(128)S(1)} all-reduce(f32[2]{0:T(128)S(1)} %broadcast_multiply_fusion.9), channel_id=1, replica_groups=mesh['member'=2,'gridy'=8,'gridx'=8] {'gridy'}, use_global_device_ids=true, to_apply=%region_34.35 | all-reduce | flops 2 | bytes 16 | tf_op jit(solution)/shard_map/psum | solution.py:156
  1696.2 5.8 all-reduce
  1705.1 7.6 all-gather.2.cloned.1.call-done
  (365 shorter events, 210.4 us)
Async XLA Ops:
  7.2 1705.5 %all-gather.2.cloned.1.call-start = ((), (), s32[]{:S(2)}) async-start(), calls=%async_computation | async-start | bytes 6291456 | tf_op jit(solution)/shard_map/all_gather | solution.py:159
  19.9 14.3 collective-permute-start.3
  23.1 12.8 collective-permute-start.2
  49.1 6.2 collective-permute-start.7
  49.2 6.9 collective-permute-start.6
  61.9 5.7 collective-permute-start.11
  62.0 5.7 collective-permute-start.10
  340.5 12.2 collective-permute-start.13
  632.1 12.2 collective-permute-start.17
  790.4 15.3 collective-permute-start.20
  790.5 15.2 collective-permute-start.21
  826.9 15.0 collective-permute-start.27
  829.4 14.9 collective-permute-start.26
  859.0 7.2 collective-permute-start.31
  859.0 7.3 collective-permute-start.30
  873.2 7.6 collective-permute-start.35
  873.2 8.2 collective-permute-start.34
  1158.9 12.5 collective-permute-start.37
  1172.5 8.1 collective-permute-start.39
  1172.7 8.0 collective-permute-start.38
  1460.6 12.6 collective-permute-start.41
  1474.3 8.2 collective-permute-start.43
  1474.3 8.2 collective-permute-start.42
  1617.8 12.3 collective-permute-start.45
  (78 other events, 753.0 us)
Sparse Core Ops, SparseCore 0:
  1646.8 65.7 all-gather.1
where the time goes:
time: 1730 us; the launch traced here: 1720 us
  blocking collectives  1410 us (82%)
  starting transfers between devices  137 us (8%)
  other arithmetic  72.2 us (4%)
  local copies, waits for them, and re-layouts  59.9 us (3%)
  waiting for transfers between devices  31 us (2%)
    psum x6, blocking collectives, squared_norm(): return lax.psum(member_total(residual * residual), ('gridy', 'gridx'))  825 us
    psum x4, blocking collectives, surface_solve(): lax.psum(member_total(direction * image), ('gridy', 'gridx'))  531 us
    ppermute x24, starting transfers between devices, padded_2(): lax.ppermute(lax.slice_in_dim(block, 0, width, axis=dim), axis, backward)  128 us
  transfers between devices with their start and end apart: 49, of which 31 were waited for; matrix products, arithmetic and copies ran while one was open for 3% of the time, Pallas kernels for 0%

commit v1 on v0

--- a/solution.py
+++ b/solution.py
@@ -1,3 +1,4 @@
+import functools
 import jax
 import jax.numpy as jnp
 from jax import lax
@@ -16,6 +17,15 @@
 SURF_C = 4.0
 DIV_K = 0.5
 GRAV_K = 0.5
+
+
+def see_cubes(z, ax_name, peer_axis):
+    for p in (ax_name, peer_axis):
+        z = jax.lax.psum(z, p)
+    return z
+
+
+move_the_keys = functools.partial(see_cubes, ax_name="gridx", peer_axis="gridy")
 
 
 def padded_2(block, sides, width):
@@ -68,7 +78,7 @@
 
 
 def squared_norm(residual):
-    return lax.psum(member_total(residual * residual), ("gridy", "gridx"))
+    return move_the_keys(member_total(residual * residual))
 
 
 def widen(values):

time: 1730 us -> 1350 us (0.78)
  blocking collectives: 1410 us -> 1070 us
  starting transfers between devices: 137 us -> 97.4 us
    psum x6 -> x12, blocking collectives: 825 us -> 237 us  [see_cubes(): z = jax.lax.psum(z, p)]
    psum x4 -> x6, blocking collectives: 531 us -> 780 us  [surface_solve(): lax.psum(member_total(direction * image), ('gridy', 'gridx'))]
    ppermute x24, starting transfers between devices: 128 us -> 86.6 us  [padded_2(): lax.ppermute(lax.slice_in_dim(block, 0, width, axis=dim), axis, backward)]
  transfers between devices with their start and end apart: 49 -> 49, of which waited for: 31 -> 29; matrix products, arithmetic and copies ran while one was open for 3% -> 4% of each run, Pallas kernels for 0% -> 0%
where the time goes in v1:
time: 1350 us
  blocking collectives  1070 us (79%)
  starting transfers between devices  97.4 us (7%)
  other arithmetic  72.3 us (5%)
  local copies, waits for them, and re-layouts  60.1 us (4%)
  waiting for transfers between devices  31.9 us (2%)
  between operations  16.3 us (1%)
    psum x6, blocking collectives, surface_solve(): lax.psum(member_total(direction * image), ('gridy', 'gridx'))  780 us
    psum x12, blocking collectives, see_cubes(): z = jax.lax.psum(z, p)  237 us
    ppermute x24, starting transfers between devices, padded_2(): lax.ppermute(lax.slice_in_dim(block, 0, width, axis=dim), axis, backward)  86.6 us
  transfers between devices with their start and end apart: 49, of which 29 were waited for; matrix products, arithmetic and copies ran while one was open for 4% of the time, Pallas kernels for 0%

profile of v1, /device:TPU:1, one launch (start us, length us, event | category | flops | bytes accessed | tf_op | source)
XLA Modules:
  0.0 1347.6 jit_solution(5584272420258410526)
XLA Ops:
  68.1 16.6 %psum.140 = f32[2]{0:T(128)S(1)} all-reduce(f32[2]{0:T(128)S(1)} %get-tuple-element.298), channel_id=1, replica_groups=mesh['member'=2,'gridy'=8,'gridx'=8] {'gridx'}, use_global_device_ids=true, to_apply=%region_4.5 | all-reduce | flops 2 | bytes 16 | tf_op jit(solution)/shard_map/psum | solution.py:24
  84.7 19.5 %psum.141 = f32[2]{0:T(128)S(1)} all-reduce(f32[2]{0:T(128)S(1)} %psum.140), channel_id=1, replica_groups=mesh['member'=2,'gridy'=8,'gridx'=8] {'gridy'}, use_global_device_ids=true, to_apply=%region_5.6 | all-reduce | flops 2 | bytes 16 | tf_op jit(solution)/shard_map/psum | solution.py:24
  104.2 127.4 %psum.142 = f32[2]{0:T(128)S(1)} all-reduce(f32[2]{0:T(128)S(1)} %get-tuple-element.297), channel_id=1, replica_groups=mesh['member'=2,'gridy'=8,'gridx'=8] {'gridy','gridx'}, use_global_device_ids=true, to_apply=%region_7.8 | all-reduce | flops 2 | bytes 16 | tf_op jit(solution)/shard_map/psum | solution.py:95
  231.7 14.0 %psum.143 = f32[2]{0:T(128)S(1)} all-reduce(f32[2]{0:T(128)S(1)} %get-tuple-element.312), channel_id=1, replica_groups=mesh['member'=2,'gridy'=8,'gridx'=8] {'gridx'}, use_global_device_ids=true, to_apply=%region_9.10 | all-reduce | flops 2 | bytes 16 | tf_op jit(solution)/shard_map/psum | solution.py:24
  245.8 27.8 %psum.144 = f32[2]{0:T(128)S(1)} all-reduce(f32[2]{0:T(128)S(1)} %psum.143), channel_id=1, replica_groups=mesh['member'=2,'gridy'=8,'gridx'=8] {'gridy'}, use_global_device_ids=true, to_apply=%region_10.11 | all-reduce | flops 2 | bytes 16 | tf_op jit(solution)/shard_map/psum | solution.py:24
  282.4 132.0 %psum.145 = f32[2]{0:T(128)S(1)} all-reduce(f32[2]{0:T(128)S(1)} %get-tuple-element.310), channel_id=1, replica_groups=mesh['member'=2,'gridy'=8,'gridx'=8] {'gridy','gridx'}, use_global_device_ids=true, to_apply=%region_12.13 | all-reduce | flops 2 | bytes 16 | tf_op jit(solution)/shard_map/psum | solution.py:95
  414.6 12.8 psum.146
  427.5 26.9 %psum.147 = f32[2]{0:T(128)S(1)} all-reduce(f32[2]{0:T(128)S(1)} %psum.146), channel_id=1, replica_groups=mesh['member'=2,'gridy'=8,'gridx'=8] {'gridy'}, use_global_device_ids=true, to_apply=%region_15.16 | all-reduce | flops 2 | bytes 16 | tf_op jit(solution)/shard_map/psum | solution.py:24
  467.9 132.4 %psum.148 = f32[2]{0:T(128)} all-reduce(f32[2]{0:T(128)} %fusion.143), channel_id=1, replica_groups=mesh['member'=2,'gridy'=8,'gridx'=8] {'gridy','gridx'}, use_global_device_ids=true, to_apply=%region_17.18 | all-reduce | flops 2 | bytes 16 | tf_op jit(solution)/shard_map/psum | solution.py:95
  602.1 11.7 collective-permute-start.21
  694.8 14.8 %psum.149 = f32[2]{0:T(128)} all-reduce(f32[2]{0:T(128)} %get-tuple-element.296), channel_id=1, replica_groups=mesh['member'=2,'gridy'=8,'gridx'=8] {'gridx'}, use_global_device_ids=true, to_apply=%region_22.23 | all-reduce | flops 2 | bytes 16 | tf_op jit(solution)/shard_map/psum | solution.py:24
  709.6 20.1 %psum.150 = f32[2]{0:T(128)} all-reduce(f32[2]{0:T(128)} %psum.149), channel_id=1, replica_groups=mesh['member'=2,'gridy'=8,'gridx'=8] {'gridy'}, use_global_device_ids=true, to_apply=%region_23.24 | all-reduce | flops 2 | bytes 16 | tf_op jit(solution)/shard_map/psum | solution.py:24
  729.7 128.0 %psum.151 = f32[2]{0:T(128)} all-reduce(f32[2]{0:T(128)} %get-tuple-element.295), channel_id=1, replica_groups=mesh['member'=2,'gridy'=8,'gridx'=8] {'gridy','gridx'}, use_global_device_ids=true, to_apply=%region_25.26 | all-reduce | flops 2 | bytes 16 | tf_op jit(solution)/shard_map/psum | solution.py:95
  859.6 14.1 %psum.152 = f32[2]{0:T(128)S(1)} all-reduce(f32[2]{0:T(128)} %get-tuple-element.303), channel_id=1, replica_groups=mesh['member'=2,'gridy'=8,'gridx'=8] {'gridx'}, use_global_device_ids=true, to_apply=%region_27.28 | all-reduce | flops 2 | bytes 16 | tf_op jit(solution)/shard_map/psum | solution.py:24
  873.7 27.9 %psum.153 = f32[2]{0:T(128)S(1)} all-reduce(f32[2]{0:T(128)S(1)} %psum.152), channel_id=1, replica_groups=mesh['member'=2,'gridy'=8,'gridx'=8] {'gridy'}, use_global_device_ids=true, to_apply=%region_28.29 | all-reduce | flops 2 | bytes 16 | tf_op jit(solution)/shard_map/psum | solution.py:24
  917.6 130.0 %psum.154 = f32[2]{0:T(128)} all-reduce(f32[2]{0:T(128)} %get-tuple-element.301), channel_id=1, replica_groups=mesh['member'=2,'gridy'=8,'gridx'=8] {'gridy','gridx'}, use_global_device_ids=true, to_apply=%region_30.31 | all-reduce | flops 2 | bytes 16 | tf_op jit(solution)/shard_map/psum | solution.py:95
  1050.4 14.2 %psum.155 = f32[2]{0:T(128)} all-reduce(f32[2]{0:T(128)} %multiply_reduce_fusion), channel_id=1, replica_groups=mesh['member'=2,'gridy'=8,'gridx'=8] {'gridx'}, use_global_device_ids=true, to_apply=%region_32.33 | all-reduce | flops 2 | bytes 16 | tf_op jit(solution)/shard_map/psum | solution.py:24
  1064.6 28.7 %psum.156 = f32[2]{0:T(128)} all-reduce(f32[2]{0:T(128)} %psum.155), channel_id=1, replica_groups=mesh['member'=2,'gridy'=8,'gridx'=8] {'gridy'}, use_global_device_ids=true, to_apply=%region_33.34 | all-reduce | flops 2 | bytes 16 | tf_op jit(solution)/shard_map/psum | solution.py:24
  1109.0 130.0 %psum.157 = f32[2]{0:T(128)} all-reduce(f32[2]{0:T(128)} %fusion.107), channel_id=1, replica_groups=mesh['member'=2,'gridy'=8,'gridx'=8] {'gridy','gridx'}, use_global_device_ids=true, to_apply=%region_35.36 | all-reduce | flops 2 | bytes 16 | tf_op jit(solution)/shard_map/psum | solution.py:95
  1240.7 11.7 collective-permute-start.45
  1271.2 16.1 %psum.158 = f32[2,4,64]{2,1,0:T(4,128)S(1)} all-reduce(f32[2,4,64]{2,1,0:T(4,128)S(1)} %copy-done.41), channel_id=1, replica_groups=mesh['member'=2,'gridy'=8,'gridx'=8] {'gridx'}, use_global_device_ids=true, to_apply=%region_37.38 | all-reduce | flops 512 | bytes 4096 | tf_op jit(solution)/shard_map/psum | solution.py:164
  1288.0 9.2 all_gather.10
  1297.2 21.4 %psum.159 = f32[2]{0:T(128)S(1)} all-reduce(f32[2]{0:T(128)S(1)} %broadcast_multiply_fusion.9), channel_id=1, replica_groups=mesh['member'=2,'gridy'=8,'gridx'=8] {'gridy'}, use_global_device_ids=true, to_apply=%region_40.41 | all-reduce | flops 2 | bytes 16 | tf_op jit(solution)/shard_map/psum | solution.py:166
  1328.2 8.0 all-gather.2.cloned.1.call-done
  (373 shorter events, 236.0 us)
Async XLA Ops:
  7.2 1329.1 %all-gather.2.cloned.1.call-start = ((), (), s32[]{:S(2)}) async-start(), calls=%async_computation | async-start | bytes 6291456 | tf_op jit(solution)/shard_map/all_gather | solution.py:169
  19.9 14.3 %collective-permute-start.3 = (f32[5,2,4,66,1]{3,2,4,1,0:T(4,128)S(1)}, f32[5,2,4,66,1]{3,2,4,1,0:T(4,128)S(1)}, u32[]{:S(2)}, u32[]{:S(2)}) collective-permute-start(f32[5,2,4,66,1]{3,2,4,1,0:T(4,128)S(1)} %copy.16), channel_id=1, source_target_pairs={{0,1},{1,2},{2,3},{3,4},{4,5},{5,6},{6,7},{7,0},{8,9},{9,10},{10,1... | collective-permute-start | bytes 31688 | tf_op jit(solution)/shard_map/ppermute | solution.py:37
  23.1 12.9 collective-permute-start.2
  49.2 6.2 collective-permute-start.7
  49.3 6.9 collective-permute-start.6
  62.0 5.7 collective-permute-start.11
  62.1 5.7 collective-permute-start.10
  276.8 5.4 collective-permute-start.15
  458.1 5.4 collective-permute-start.19
  602.1 15.2 %collective-permute-start.20 = (f32[1,2,1,256]{3,2,1,0:T(1,128)S(1)}, f32[1,2,1,256]{3,2,1,0:T(1,128)S(1)}, u32[]{:S(2)}, u32[]{:S(2)}) collective-permute-start(f32[1,2,1,256]{3,2,1,0:T(1,128)S(1)} %get-tuple-element.389), channel_id=1, source_target_pairs={{0,8},{8,16},{16,24},{24,32},{32,40},{40,48},{48,56},{56,0},{1,9},... | collective-permute-start | bytes 6152 | tf_op jit(solution)/shard_map/ppermute | solution.py:37
  602.1 15.2 %collective-permute-start.21 = (f32[1,2,1,256]{3,2,1,0:T(1,128)S(1)}, f32[1,2,1,256]{3,2,1,0:T(1,128)S(1)}, u32[]{:S(2)}, u32[]{:S(2)}) collective-permute-start(f32[1,2,1,256]{3,2,1,0:T(1,128)S(1)} %get-tuple-element.390), channel_id=1, source_target_pairs={{8,0},{16,8},{24,16},{32,24},{40,32},{48,40},{56,48},{0,56},{9,1},... | collective-permute-start | bytes 6152 | tf_op jit(solution)/shard_map/ppermute | solution.py:40
  617.4 5.4 collective-permute-start.23
  617.5 5.4 collective-permute-start.22
  638.5 15.0 %collective-permute-start.27 = (f32[5,2,4,66,1]{3,2,4,1,0:T(4,128)}, f32[5,2,4,66,1]{3,2,4,1,0:T(4,128)}, u32[]{:S(2)}, u32[]{:S(2)}) collective-permute-start(f32[5,2,4,66,1]{3,2,4,1,0:T(4,128)} %copy.20), channel_id=1, source_target_pairs={{0,1},{1,2},{2,3},{3,4},{4,5},{5,6},{6,7},{7,0},{8,9},{9,10},{10,1... | collective-permute-start | bytes 31688 | tf_op jit(solution)/shard_map/ppermute | solution.py:37
  641.0 14.9 %collective-permute-start.26 = (f32[5,2,4,66,1]{3,2,4,1,0:T(4,128)}, f32[5,2,4,66,1]{3,2,4,1,0:T(4,128)}, u32[]{:S(2)}, u32[]{:S(2)}) collective-permute-start(f32[5,2,4,66,1]{3,2,4,1,0:T(4,128)} %copy.18), channel_id=1, source_target_pairs={{1,0},{2,1},{3,2},{4,3},{5,4},{6,5},{7,6},{0,7},{9,8},{10,9},{11,1... | collective-permute-start | bytes 31688 | tf_op jit(solution)/shard_map/ppermute | solution.py:40
  670.6 7.3 collective-permute-start.31
  670.6 7.3 collective-permute-start.30
  684.8 7.5 collective-permute-start.35
  684.8 8.1 collective-permute-start.34
  907.0 8.2 collective-permute-start.39
  907.0 8.2 collective-permute-start.38
  1098.9 8.2 collective-permute-start.43
  1098.9 8.2 collective-permute-start.42
  1240.7 12.6 collective-permute-start.45
  (78 other events, 524.8 us)
Sparse Core Ops, SparseCore 0:
  1270.0 66.2 all-gather.1
